TPU v7x, 32 devices: a whole 2x2x4 slice. The times are simulated.
32 devices in a mesh: energy: 8 (over z, x), slab: 2 (over core), rep: 2 (over y).
Axes of the slice: x: 2, y: 2, z: 4, core: 2. Of those that a mesh axis runs over, the one named last changes fastest.
Arguments:
- green_blocks: bfloat16 [8, 2, 512, 512], P('energy', 'slab', 'rep'), may hold values from -1 to 1
- occupation: float32 [8], P('energy'), may hold values from 0.1 to 1
- offsets: int32 [2], replicated, may hold values from 1 to 4, as said below
- coulomb: float32 [2, 512, 512], P('slab', 'rep'), may hold values from -0.9 to 0.9
- hamiltonian: float32 [2, 512, 512], P('slab', 'rep'), may hold values from -0.25 to 0.25
- onsite_level: float32 [8], P('energy'), may hold values from 2 to 3
- green_steps: int32 [8], P('energy'), may hold values from 1 to 2, as said below
- screen_steps: int32 [2], replicated, may hold values from 0 to 2, as said below
Outputs:
- green_next: float32 [8, 2, 512, 512], P('energy', 'slab', 'rep')
- screened: bfloat16 [2, 2, 512, 512], P(None, 'slab', 'rep')
Inputs may be any that keep to these rules, and one draw needn't show every extreme that they name: `offsets`: some frequency has offset 4; every other frequency has a smaller one. `green_steps`: some energy takes 2 turns. `screen_steps`: some frequency takes 2 turns; every other frequency takes fewer.
All inputs are finite; a program needn't handle non-finite values.
Results may differ from a plain program's by a relative error of at most 0.0004.
Values may be sent and summed in bfloat16 or wider, within the bound.
No kernel may reach another device: no remote copies, remote signals or barrier semaphores. Data moves between devices by JAX's collectives and lax.ppermute only.
A program may use at most 64 MiB of HBM per device.

v0:
```python
import jax
import jax.numpy as jnp
from jax import lax
from jax.sharding import PartitionSpec as P

SHIFTS = 4
FREQS = 2
NG = 2
NW = 2
precise = lax.Precision.HIGHEST


def from_behind(block, axis, distance):
    devices = range(lax.axis_size(axis))
    route = [(i - distance, i) for i in devices if i - distance in devices]
    return lax.ppermute(block, axis, route)


def broadcast(block, axis, owner):
    block = jnp.where(lax.axis_index(axis) == owner, block, jnp.zeros_like(block))
    return lax.psum(block, axis)


def with_halo(value, sides, width):
    for axis, dim in sides:
        peers, length = (lax.axis_size(axis), value.shape[dim])
        up = [(i, (i + 1) % peers) for i in range(peers - 1)]
        down = [(j, i) for i, j in up]
        last = lax.slice_in_dim(value, length - width, length, axis=dim)
        first = lax.slice_in_dim(value, 0, width, axis=dim)
        before = lax.ppermute(last, axis, up)
        after = lax.ppermute(first, axis, down)
        value = jnp.concatenate([before, value, after], axis=dim)
    return value


def row_product(first_factor, second_factor):
    return jnp.einsum("esij,esjk->esik", first_factor, second_factor, precision=precise)


def full_rows(block_rows):
    return lax.all_gather(block_rows, "rep", axis=2, tiled=True)


def newton_rows(operator, initial, known_full, counts, turn_total):
    operator_full = lax.all_gather(operator, "rep", axis=2, tiled=True)
    iterate = initial
    for turn_index in range(turn_total):
        if turn_index == 0 and known_full is not None:
            iterate_full = known_full
        else:
            iterate_full = full_rows(iterate)
        composed = row_product(row_product(iterate, operator_full), iterate_full)
        iterate = jnp.where(
            (turn_index < counts)[:, None, None, None], 2.0 * iterate - composed, iterate
        )
    return iterate


def body(
    green_blocks, occupation, offsets, coulomb, hamiltonian, onsite_level, green_steps, screen_steps
):
    local_count, _, half_rows, full_width = green_blocks.shape
    energies = local_count * lax.axis_size("energy")
    entry_scale = full_width ** (-0.5)
    shift_count = -(-SHIFTS // local_count)
    pieces = []
    received = green_blocks
    for distance in range(1, shift_count + 1):
        received = from_behind(received, "energy", 1)
        pieces.insert(0, received)
    extended = jnp.concatenate(pieces + [green_blocks], axis=0)
    anchor = shift_count * local_count
    lowered = jnp.stack(
        [
            lax.dynamic_slice_in_dim(extended, anchor - offsets[index], local_count, 0)
            for index in range(FREQS)
        ]
    )
    lowered_wide = lowered.astype(jnp.float32)
    weighted = occupation[:, None, None, None] * green_blocks.astype(jnp.float32)
    partial_value = jnp.sum(weighted[None] * lowered_wide, axis=1) * energies ** (-0.5)
    polarization = lax.psum(partial_value, "energy")
    rep_start = lax.axis_index("rep") * half_rows
    col_index = lax.broadcasted_iota(jnp.int32, (half_rows, full_width), 1)
    row_index = lax.broadcasted_iota(jnp.int32, (half_rows, full_width), 0) + rep_start
    identity_rows = (col_index == row_index).astype(jnp.float32)
    identity_full = jnp.eye(full_width, dtype=jnp.float32)[None, None]
    owner_index = lax.axis_index("energy") % FREQS
    polar_own = lax.dynamic_index_in_dim(polarization, owner_index, 0, keepdims=True)
    screen_operator = identity_rows + entry_scale * coulomb[None] * polar_own
    count_own = lax.dynamic_index_in_dim(screen_steps, owner_index, 0, keepdims=True)
    screen_start = jnp.broadcast_to(identity_rows, screen_operator.shape)
    inverse = newton_rows(screen_operator, screen_start, identity_full, count_own, NW)
    inverse_full = full_rows(inverse)
    screened_own = row_product(coulomb[None], inverse_full).astype(jnp.bfloat16)
    screened = jnp.stack([broadcast(screened_own, "energy", index)[0] for index in range(FREQS)])
    self_energy = (
        jnp.sum(lowered_wide * screened.astype(jnp.float32)[:, None], axis=0) * entry_scale
    )
    neighbours = with_halo(green_blocks, (("slab", 1),), 1)
    contact = (neighbours[:, 0:1].astype(jnp.float32) + neighbours[:, 2:3].astype(jnp.float32)) * (
        0.5 * entry_scale
    )
    dyson_rows = (
        onsite_level[:, None, None, None] * identity_rows
        + hamiltonian[None]
        - self_energy
        - contact
    )
    diagonal = jnp.sum(dyson_rows * identity_rows, axis=-1)
    initial = identity_rows * (1.0 / diagonal)[..., None]
    green_next = newton_rows(dyson_rows, initial, None, green_steps, NG)
    return (green_next, screened)


def solution(mesh):
    return jax.shard_map(
        body,
        mesh=mesh,
        in_specs=(
            P("energy", "slab", "rep", None),
            P("energy"),
            P(),
            P("slab", "rep", None),
            P("slab", "rep", None),
            P("energy"),
            P("energy"),
            P(),
        ),
        out_specs=(P("energy", "slab", "rep", None), P(None, "slab", "rep", None)),
        check_vma=False,
    )
```

profile of v0, /device:TPU:0, one launch (start us, length us, event | category | flops | bytes accessed | tf_op | source)
XLA Modules:
  0.0 359.1 jit_solution(1811731379270840315)
XLA Ops:
  7.2 1.1 copy.17
  8.3 4.9 %collective-permute-start = (bf16[1,1,256,512]{2,3,1,0:T(8,128)(2,1)S(1)}, bf16[1,1,256,512]{2,3,1,0:T(8,128)(2,1)S(1)}, u32[]{:S(2)}, u32[]{:S(2)}) collective-permute-start(bf16[1,1,256,512]{2,3,1,0:T(8,128)(2,1)S(1)} %copy.17), channel_id=1, source_target_pairs={{0,4},{4,8},{8,12},{12,16},{16,20},{20,24},{24,28},{1,5},{5,9},{9,... | collective-permute-start | bytes 786440 | tf_op jit(solution)/shard_map/ppermute | solution.py:16
  13.2 5.5 %collective-permute-done = bf16[1,1,256,512]{2,3,1,0:T(8,128)(2,1)S(1)} collective-permute-done((bf16[1,1,256,512]{2,3,1,0:T(8,128)(2,1)S(1)}, bf16[1,1,256,512]{2,3,1,0:T(8,128)(2,1)S(1)}, u32[]{:S(2)}, u32[]{:S(2)}) %collective-permute-start) | collective-permute-done | bytes 262176 | tf_op jit(solution)/shard_map/ppermute | solution.py:16
  18.7 4.4 %collective-permute-start.1 = (bf16[1,1,256,512]{2,3,1,0:T(8,128)(2,1)S(1)}, bf16[1,1,256,512]{2,3,1,0:T(8,128)(2,1)S(1)}, u32[]{:S(2)}, u32[]{:S(2)}) collective-permute-start(bf16[1,1,256,512]{2,3,1,0:T(8,128)(2,1)S(1)} %collective-permute-done), channel_id=1, source_target_pairs={{0,4},{4,8},{8,12},{12,16},{16,20},{20,24},{24,28},{1,5},{5,9},{9,... | collective-permute-start | bytes 786440 | tf_op jit(solution)/shard_map/ppermute | solution.py:16
  23.1 4.7 %collective-permute-done.1 = bf16[1,1,256,512]{2,3,1,0:T(8,128)(2,1)S(1)} collective-permute-done((bf16[1,1,256,512]{2,3,1,0:T(8,128)(2,1)S(1)}, bf16[1,1,256,512]{2,3,1,0:T(8,128)(2,1)S(1)}, u32[]{:S(2)}, u32[]{:S(2)}) %collective-permute-start.1) | collective-permute-done | bytes 262176 | tf_op jit(solution)/shard_map/ppermute | solution.py:16
  27.8 4.4 %collective-permute-start.2 = (bf16[1,1,256,512]{2,3,1,0:T(8,128)(2,1)S(1)}, bf16[1,1,256,512]{2,3,1,0:T(8,128)(2,1)S(1)}, u32[]{:S(2)}, u32[]{:S(2)}) collective-permute-start(bf16[1,1,256,512]{2,3,1,0:T(8,128)(2,1)S(1)} %collective-permute-done.1), channel_id=1, source_target_pairs={{0,4},{4,8},{8,12},{12,16},{16,20},{20,24},{24,28},{1,5},{5,9},{9,... | collective-permute-start | bytes 786440 | tf_op jit(solution)/shard_map/ppermute | solution.py:16
  32.2 3.9 %collective-permute-done.2 = bf16[1,1,256,512]{2,3,1,0:T(8,128)(2,1)S(1)} collective-permute-done((bf16[1,1,256,512]{2,3,1,0:T(8,128)(2,1)S(1)}, bf16[1,1,256,512]{2,3,1,0:T(8,128)(2,1)S(1)}, u32[]{:S(2)}, u32[]{:S(2)}) %collective-permute-start.2) | collective-permute-done | bytes 262176 | tf_op jit(solution)/shard_map/ppermute | solution.py:16
  36.1 5.3 %collective-permute-start.3 = (bf16[1,1,256,512]{2,3,1,0:T(8,128)(2,1)S(1)}, bf16[1,1,256,512]{2,3,1,0:T(8,128)(2,1)S(1)}, u32[]{:S(2)}, u32[]{:S(2)}) collective-permute-start(bf16[1,1,256,512]{2,3,1,0:T(8,128)(2,1)S(1)} %collective-permute-done.2), channel_id=1, source_target_pairs={{0,4},{4,8},{8,12},{12,16},{16,20},{20,24},{24,28},{1,5},{5,9},{9,... | collective-permute-start | bytes 786440 | tf_op jit(solution)/shard_map/ppermute | solution.py:16
  41.3 1.3 fusion.24
  45.9 1.0 multiply_bitcast_fusion
  46.9 0.2 copy.20
  47.3 1.1 multiply_multiply_fusion
  48.4 0.0 all-gather.10.cloned.1.call-start
  48.5 0.2 copy.19
  48.7 80.2 %all-reduce.4.cloned.1.call-done = f32[2,1,256,512]{2,3,1,0:T(8,128)} async-done(((f32[2,1,256,512]{2,3,1,0:T(8,128)}), f32[2,1,256,512]{2,3,1,0:T(8,128)}) %all-reduce.4.cloned.1.call-update) | async-done | bytes 1048592 | tf_op jit(solution)/shard_map/psum | solution.py:83
  129.0 1.9 fusion.18
  130.9 0.0 all-gather.16.cloned.1.call-start
  131.0 0.6 dynamic_slice.16
  132.2 19.8 %all-gather.10.cloned.1.call-done = f32[1,1,512,512]{2,3,1,0:T(8,128)} async-done(((f32[1,1,256,512]{2,3,1,0:T(8,128)}), f32[1,1,512,512]{2,3,1,0:T(8,128)}) %all-gather.10.cloned.1.call-update) | async-done | bytes 1048592 | tf_op jit(solution)/shard_map/all_gather | solution.py:46
  152.0 2.0 fusion.12
  154.0 1.4 fusion.4
  155.4 0.0 all-gather.18.cloned.1.call-start
  156.2 2.1 fusion.10
  158.3 18.6 %all-gather.16.cloned.1.call-done = f32[512,512]{1,0:T(8,128)} async-done(((f32[256,512]{1,0:T(8,128)}), f32[512,512]{1,0:T(8,128)}) %all-gather.16.cloned.1.call-update) | async-done | bytes 1048592 | tf_op jit(solution)/shard_map/all_gather | solution.py:42
  176.8 3.1 fusion
  179.9 0.0 all-reduce.6.cloned.1.call-start
  180.0 21.4 %all-gather.18.cloned.1.call-done = f32[512,512]{1,0:T(8,128)} async-done(((f32[256,512]{1,0:T(8,128)}), f32[512,512]{1,0:T(8,128)}) %all-gather.18.cloned.1.call-update) | async-done | bytes 1048592 | tf_op jit(solution)/shard_map/all_gather | solution.py:42
  201.4 3.8 %select_bitcast_fusion.1 = (bf16[1,1,256,512]{2,3,1,0:T(8,128)(2,1)}, bf16[1,1,256,512]{2,3,1,0:T(8,128)(2,1)}) fusion(pred[]{:T(512)S(6)} %eq.72, pred[]{:T(512)S(6)} %eq.76, f32[512,512]{1,0:T(8,128)} %all-gather.18.cloned.1.call-done, f32[1,256,512]{2,1,0:T(8,128)S(1)} %copy-done.4), kind=kOutput, calls=%fused_computation.41 | convolution fusion | flops 805699584 | bytes 2097154 | tf_op jit(solution)/shard_map/esij,esjk->esik/dot_general | solution.py:38
  205.3 1.6 collective-permute-start.4
  206.9 1.3 collective-permute-start.5
  208.2 0.2 copy.16
  209.0 69.2 %all-reduce.6.cloned.1.call-done = (bf16[1,1,256,512]{2,3,1,0:T(8,128)(2,1)}, bf16[1,1,256,512]{2,3,1,0:T(8,128)(2,1)}) async-done(((bf16[1,1,256,512]{2,3,1,0:T(8,128)(2,1)}, bf16[1,1,256,512]{2,3,1,0:T(8,128)(2,1)}), (bf16[1,1,256,512]{2,3,1,0:T(8,128)(2,1)}, bf16[1,1,256,512]{2,3,1,0:T(8,128)(2,1)})) %all-reduce.6.cloned.1.call-update) | async-done | bytes 524304 | tf_op jit(solution)/shard_map/psum | solution.py:21
  278.2 1.2 multiply_reduce_fusion
  279.5 1.0 select_reduce_fusion
  280.5 0.0 all-gather.14.cloned.1.call-start
  280.6 0.8 fusion.19
  281.4 0.2 all-gather.20.cloned.1.call-start
  282.3 1.1 compare_select_fusion
  283.4 17.7 %all-gather.12.cloned.1.call-done = f32[1,1,512,512]{2,3,1,0:T(8,128)} async-done(((f32[1,1,256,512]{2,3,1,0:T(8,128)}), f32[1,1,512,512]{2,3,1,0:T(8,128)}) %all-gather.12.cloned.1.call-update) | async-done | bytes 1048592 | tf_op jit(solution)/shard_map/all_gather | solution.py:46
  301.1 2.3 fusion.8
  303.4 21.1 %all-gather.14.cloned.1.call-done = f32[1,1,512,512]{2,3,1,0:T(8,128)} async-done(((f32[1,1,256,512]{2,3,1,0:T(8,128)}), f32[1,1,512,512]{2,3,1,0:T(8,128)}) %all-gather.14.cloned.1.call-update) | async-done | bytes 1048592 | tf_op jit(solution)/shard_map/all_gather | solution.py:42
  324.6 3.2 fusion.1
  327.8 0.1 pad_maximum_fusion
  327.8 1.0 copy.23
  328.8 0.5 copy-done.2
  329.3 1.1 fusion.6
  330.4 18.8 %all-gather.20.cloned.1.call-done = f32[512,512]{1,0:T(8,128)} async-done(((f32[256,512]{1,0:T(8,128)}), f32[512,512]{1,0:T(8,128)}) %all-gather.20.cloned.1.call-update) | async-done | bytes 1048592 | tf_op jit(solution)/shard_map/all_gather | solution.py:42
  349.2 3.1 fusion.3
  (38 shorter events, 0.4 us)
Async XLA Ops:
  7.2 121.8 %all-reduce.4.cloned.1.call-start = ((), (), s32[]{:S(2)}) async-start(), calls=%async_computation | async-start | bytes 2097152 | tf_op jit(solution)/shard_map/psum | solution.py:83
  8.3 10.4 %collective-permute-start = (bf16[1,1,256,512]{2,3,1,0:T(8,128)(2,1)S(1)}, bf16[1,1,256,512]{2,3,1,0:T(8,128)(2,1)S(1)}, u32[]{:S(2)}, u32[]{:S(2)}) collective-permute-start(bf16[1,1,256,512]{2,3,1,0:T(8,128)(2,1)S(1)} %copy.17), channel_id=1, source_target_pairs={{0,4},{4,8},{8,12},{12,16},{16,20},{20,24},{24,28},{1,5},{5,9},{9,... | collective-permute-start | bytes 786440 | tf_op jit(solution)/shard_map/ppermute | solution.py:16
  18.7 9.1 %collective-permute-start.1 = (bf16[1,1,256,512]{2,3,1,0:T(8,128)(2,1)S(1)}, bf16[1,1,256,512]{2,3,1,0:T(8,128)(2,1)S(1)}, u32[]{:S(2)}, u32[]{:S(2)}) collective-permute-start(bf16[1,1,256,512]{2,3,1,0:T(8,128)(2,1)S(1)} %collective-permute-done), channel_id=1, source_target_pairs={{0,4},{4,8},{8,12},{12,16},{16,20},{20,24},{24,28},{1,5},{5,9},{9,... | collective-permute-start | bytes 786440 | tf_op jit(solution)/shard_map/ppermute | solution.py:16
  27.8 8.3 %collective-permute-start.2 = (bf16[1,1,256,512]{2,3,1,0:T(8,128)(2,1)S(1)}, bf16[1,1,256,512]{2,3,1,0:T(8,128)(2,1)S(1)}, u32[]{:S(2)}, u32[]{:S(2)}) collective-permute-start(bf16[1,1,256,512]{2,3,1,0:T(8,128)(2,1)S(1)} %collective-permute-done.1), channel_id=1, source_target_pairs={{0,4},{4,8},{8,12},{12,16},{16,20},{20,24},{24,28},{1,5},{5,9},{9,... | collective-permute-start | bytes 786440 | tf_op jit(solution)/shard_map/ppermute | solution.py:16
  36.1 11.1 %collective-permute-start.3 = (bf16[1,1,256,512]{2,3,1,0:T(8,128)(2,1)S(1)}, bf16[1,1,256,512]{2,3,1,0:T(8,128)(2,1)S(1)}, u32[]{:S(2)}, u32[]{:S(2)}) collective-permute-start(bf16[1,1,256,512]{2,3,1,0:T(8,128)(2,1)S(1)} %collective-permute-done.2), channel_id=1, source_target_pairs={{0,4},{4,8},{8,12},{12,16},{16,20},{20,24},{24,28},{1,5},{5,9},{9,... | collective-permute-start | bytes 786440 | tf_op jit(solution)/shard_map/ppermute | solution.py:16
  47.3 1.2 copy-start.4
  48.4 103.6 %all-gather.10.cloned.1.call-start = ((), (), s32[]{:S(2)}) async-start(), calls=%async_computation.1 | async-start | bytes 1572864 | tf_op jit(solution)/shard_map/all_gather | solution.py:46
  48.7 82.3 %copy-start.8 = (s32[2]{0:T(128)S(1)}, s32[2]{0:T(128)}, u32[]{:S(2)}) copy-start(s32[2]{0:T(128)} %param.15) | copy-start | bytes 28
  130.9 45.9 %all-gather.16.cloned.1.call-start = ((), (), s32[]{:S(2)}) async-start(), calls=%async_computation.4 | async-start | bytes 1572864 | tf_op jit(solution)/shard_map/all_gather | solution.py:42
  154.0 2.2 copy-start.3
  155.4 21.5 %copy-start.1 = (f32[256,512]{1,0:T(8,128)S(1)}, f32[256,512]{1,0:T(8,128)}, u32[]{:S(2)}) copy-start(f32[256,512]{1,0:T(8,128)} %fusion.4) | copy-start | bytes 1572868
  155.4 46.0 %all-gather.18.cloned.1.call-start = ((), (), s32[]{:S(2)}) async-start(), calls=%async_computation.5 | async-start | bytes 1572864 | tf_op jit(solution)/shard_map/all_gather | solution.py:42
  179.9 98.3 %all-reduce.6.cloned.1.call-start = ((), (), s32[]{:S(2)}) async-start(), calls=%async_computation.7 | async-start | bytes 1048576 | tf_op jit(solution)/shard_map/psum | solution.py:21
  180.0 28.2 %copy-start.7 = (f32[1,256,512]{2,1,0:T(8,128)S(1)}, f32[1,256,512]{2,1,0:T(8,128)}, u32[]{:S(2)}) copy-start(f32[1,256,512]{2,1,0:T(8,128)} %param.12) | copy-start | bytes 1572868
  205.2 95.9 %all-gather.12.cloned.1.call-start = ((), (), s32[]{:S(2)}) async-start(), calls=%async_computation.2 | async-start | bytes 1572864 | tf_op jit(solution)/shard_map/all_gather | solution.py:46
  205.3 74.2 %collective-permute-start.4 = (bf16[1,1,256,512]{2,3,1,0:T(8,128)(2,1)S(1)}, bf16[1,1,256,512]{2,3,1,0:T(8,128)(2,1)S(1)}, u32[]{:S(2)}, u32[]{:S(2)}) collective-permute-start(bf16[1,1,256,512]{2,3,1,0:T(8,128)(2,1)S(1)} %copy.17), channel_id=1, source_target_pairs={{0,2},{1,3},{4,6},{5,7},{8,10},{9,11},{12,14},{13,15},{16,18},{17,... | collective-permute-start | bytes 786440 | tf_op jit(solution)/shard_map/ppermute | solution.py:31
  206.9 72.6 %collective-permute-start.5 = (bf16[1,1,256,512]{2,3,1,0:T(8,128)(2,1)S(1)}, bf16[1,1,256,512]{2,3,1,0:T(8,128)(2,1)S(1)}, u32[]{:S(2)}, u32[]{:S(2)}) collective-permute-start(bf16[1,1,256,512]{2,3,1,0:T(8,128)(2,1)S(1)} %copy.17), channel_id=1, source_target_pairs={{2,0},{3,1},{6,4},{7,5},{10,8},{11,9},{14,12},{15,13},{18,16},{19,... | collective-permute-start | bytes 786440 | tf_op jit(solution)/shard_map/ppermute | solution.py:32
  280.5 44.1 %all-gather.14.cloned.1.call-start = ((), (), s32[]{:S(2)}) async-start(), calls=%async_computation.3 | async-start | bytes 1572864 | tf_op jit(solution)/shard_map/all_gather | solution.py:42
  281.4 67.8 %all-gather.20.cloned.1.call-start = ((), (), s32[]{:S(2)}) async-start(), calls=%async_computation.6 | async-start | bytes 1572864 | tf_op jit(solution)/shard_map/all_gather | solution.py:42
  324.6 3.2 copy-start.5
  324.6 3.2 copy-start.6
  327.7 1.1 copy-start
  327.7 1.6 copy-start.2
Sparse Core Ops, SparseCore 0:
  48.5 80.3 all-reduce.3
  131.1 20.8 all-gather.9
  155.5 21.2 all-gather.15
  180.1 21.2 all-gather.17
  205.3 72.8 all-reduce.5
  280.6 20.4 all-gather.11
  303.2 21.2 all-gather.13
  327.9 21.2 all-gather.19
where the time goes:
time: 360 us; the launch traced here: 359 us
  waiting for transfers between devices  281 us (78%)
  starting transfers between devices  22.3 us (6%)
  matrix products  21.9 us (6%)
  between operations  20.4 us (6%)
  other arithmetic  8.24 us (2%)
  local copies, waits for them, and re-layouts  5.22 us (1%)
    psum x1, waiting for transfers between devices, body(): polarization = lax.psum(partial_value, 'energy')  80.2 us
    all_gather x4, waiting for transfers between devices, full_rows(): return lax.all_gather(block_rows, 'rep', axis=2, tiled=True)  79.9 us
    psum x1, waiting for transfers between devices, broadcast(): return lax.psum(block, axis)  69.2 us
    all_gather x2, waiting for transfers between devices, newton_rows(): operator_full = lax.all_gather(operator, 'rep', axis=2, tiled=True)  37.5 us
    dot_general x9, matrix products, row_product(): jnp.einsum('esij,esjk->esik', first_factor, second_factor, precision=prec...  21.9 us
    ppermute x4, starting transfers between devices, from_behind(): return lax.ppermute(block, axis, route)  18.9 us
    ppermute x4, waiting for transfers between devices, from_behind(): return lax.ppermute(block, axis, route)  14.1 us
  transfers between devices with their start and end apart: 14, of which 11 were waited for; matrix products, arithmetic and copies ran while one was open for 4% of the time, Pallas kernels for 0%

commit v1 on v0

--- a/solution.py
+++ b/solution.py
@@ -8,6 +8,18 @@
 NG = 2
 NW = 2
 precise = lax.Precision.HIGHEST
+
+
+def collect(x, axis, dim):
+    ways, here, step = (lax.axis_size(axis), lax.axis_index(axis), x.shape[dim])
+    line, have = (x, 1)
+    while have < ways:
+        line = jnp.concatenate(
+            [line, lax.ppermute(line, axis, [(d, (d - have) % ways) for d in range(ways)])],
+            axis=dim,
+        )
+        have = 2 * have
+    return jnp.roll(line, here * step, axis=dim)
 
 
 def from_behind(block, axis, distance):
@@ -39,7 +51,7 @@
 
 
 def full_rows(block_rows):
-    return lax.all_gather(block_rows, "rep", axis=2, tiled=True)
+    return collect(block_rows, "rep", 2)
 
 
 def newton_rows(operator, initial, known_full, counts, turn_total):

time: 360 us -> 311 us (0.86)
  waiting for transfers between devices: 281 us -> 237 us
  matrix products: 21.9 us -> 14.5 us
    all_gather x4 -> x0, waiting for transfers between devices: 79.9 us -> none  [full_rows(): return lax.all_gather(block_rows, 'rep', axis=2, tiled=True)]
    ppermute x0 -> x4, waiting for transfers between devices: none -> 33.7 us  [collect(): lax.ppermute(line, axis, [(d, (d - have) % ways) for d in range(ways)])]
    dot_general x9, matrix products: 21.9 us -> 14.5 us  [row_product(): jnp.einsum('esij,esjk->esik', first_factor, second_factor, precision=prec...]
    ppermute x0 -> x4, starting transfers between devices: none -> 4.09 us  [collect(): lax.ppermute(line, axis, [(d, (d - have) % ways) for d in range(ways)])]
  transfers between devices with their start and end apart: 14 -> 14, of which waited for: 11 -> 10; matrix products, arithmetic and copies ran while one was open for 4% -> 4% of each run, Pallas kernels for 0% -> 0%
where the time goes in v1:
time: 311 us; the launch traced here: 310 us
  waiting for transfers between devices  237 us (76%)
  starting transfers between devices  25.9 us (8%)
  between operations  20 us (6%)
  matrix products  14.5 us (5%)
  other arithmetic  7.45 us (2%)
  local copies, waits for them, and re-layouts  4.75 us (2%)
    psum x1, waiting for transfers between devices, body(): polarization = lax.psum(partial_value, 'energy')  80.2 us
    psum x1, waiting for transfers between devices, broadcast(): return lax.psum(block, axis)  69.3 us
    all_gather x2, waiting for transfers between devices, newton_rows(): operator_full = lax.all_gather(operator, 'rep', axis=2, tiled=True)  40 us
    ppermute x4, waiting for transfers between devices, collect(): lax.ppermute(line, axis, [(d, (d - have) % ways) for d in range(ways)])  33.7 us
    ppermute x4, starting transfers between devices, from_behind(): return lax.ppermute(block, axis, route)  18.9 us
    dot_general x9, matrix products, row_product(): jnp.einsum('esij,esjk->esik', first_factor, second_factor, precision=prec...  14.5 us
    ppermute x4, waiting for transfers between devices, from_behind(): return lax.ppermute(block, axis, route)  14.1 us
  transfers between devices with their start and end apart: 14, of which 10 were waited for; matrix products, arithmetic and copies ran while one was open for 4% of the time, Pallas kernels for 0%

profile of v1, /device:TPU:0, one launch (start us, length us, event | category | flops | bytes accessed | tf_op | source)
XLA Modules:
  0.0 310.0 jit_solution(5210526853564843862)
XLA Ops:
  7.2 0.0 all-reduce.4.cloned.1.call-start
  7.2 1.1 copy.17
  8.3 4.9 %collective-permute-start = (bf16[1,1,256,512]{2,3,1,0:T(8,128)(2,1)S(1)}, bf16[1,1,256,512]{2,3,1,0:T(8,128)(2,1)S(1)}, u32[]{:S(2)}, u32[]{:S(2)}) collective-permute-start(bf16[1,1,256,512]{2,3,1,0:T(8,128)(2,1)S(1)} %copy.17), channel_id=1, source_target_pairs={{0,4},{4,8},{8,12},{12,16},{16,20},{20,24},{24,28},{1,5},{5,9},{9,... | collective-permute-start | bytes 786440 | tf_op jit(solution)/shard_map/ppermute | solution.py:28
  13.2 5.5 %collective-permute-done = bf16[1,1,256,512]{2,3,1,0:T(8,128)(2,1)S(1)} collective-permute-done((bf16[1,1,256,512]{2,3,1,0:T(8,128)(2,1)S(1)}, bf16[1,1,256,512]{2,3,1,0:T(8,128)(2,1)S(1)}, u32[]{:S(2)}, u32[]{:S(2)}) %collective-permute-start) | collective-permute-done | bytes 262176 | tf_op jit(solution)/shard_map/ppermute | solution.py:28
  18.7 4.4 %collective-permute-start.1 = (bf16[1,1,256,512]{2,3,1,0:T(8,128)(2,1)S(1)}, bf16[1,1,256,512]{2,3,1,0:T(8,128)(2,1)S(1)}, u32[]{:S(2)}, u32[]{:S(2)}) collective-permute-start(bf16[1,1,256,512]{2,3,1,0:T(8,128)(2,1)S(1)} %collective-permute-done), channel_id=1, source_target_pairs={{0,4},{4,8},{8,12},{12,16},{16,20},{20,24},{24,28},{1,5},{5,9},{9,... | collective-permute-start | bytes 786440 | tf_op jit(solution)/shard_map/ppermute | solution.py:28
  23.1 4.7 %collective-permute-done.1 = bf16[1,1,256,512]{2,3,1,0:T(8,128)(2,1)S(1)} collective-permute-done((bf16[1,1,256,512]{2,3,1,0:T(8,128)(2,1)S(1)}, bf16[1,1,256,512]{2,3,1,0:T(8,128)(2,1)S(1)}, u32[]{:S(2)}, u32[]{:S(2)}) %collective-permute-start.1) | collective-permute-done | bytes 262176 | tf_op jit(solution)/shard_map/ppermute | solution.py:28
  27.8 4.4 %collective-permute-start.2 = (bf16[1,1,256,512]{2,3,1,0:T(8,128)(2,1)S(1)}, bf16[1,1,256,512]{2,3,1,0:T(8,128)(2,1)S(1)}, u32[]{:S(2)}, u32[]{:S(2)}) collective-permute-start(bf16[1,1,256,512]{2,3,1,0:T(8,128)(2,1)S(1)} %collective-permute-done.1), channel_id=1, source_target_pairs={{0,4},{4,8},{8,12},{12,16},{16,20},{20,24},{24,28},{1,5},{5,9},{9,... | collective-permute-start | bytes 786440 | tf_op jit(solution)/shard_map/ppermute | solution.py:28
  32.2 3.9 %collective-permute-done.2 = bf16[1,1,256,512]{2,3,1,0:T(8,128)(2,1)S(1)} collective-permute-done((bf16[1,1,256,512]{2,3,1,0:T(8,128)(2,1)S(1)}, bf16[1,1,256,512]{2,3,1,0:T(8,128)(2,1)S(1)}, u32[]{:S(2)}, u32[]{:S(2)}) %collective-permute-start.2) | collective-permute-done | bytes 262176 | tf_op jit(solution)/shard_map/ppermute | solution.py:28
  36.1 5.3 %collective-permute-start.3 = (bf16[1,1,256,512]{2,3,1,0:T(8,128)(2,1)S(1)}, bf16[1,1,256,512]{2,3,1,0:T(8,128)(2,1)S(1)}, u32[]{:S(2)}, u32[]{:S(2)}) collective-permute-start(bf16[1,1,256,512]{2,3,1,0:T(8,128)(2,1)S(1)} %collective-permute-done.2), channel_id=1, source_target_pairs={{0,4},{4,8},{8,12},{12,16},{16,20},{20,24},{24,28},{1,5},{5,9},{9,... | collective-permute-start | bytes 786440 | tf_op jit(solution)/shard_map/ppermute | solution.py:28
  41.3 1.3 fusion.56
  45.9 1.0 multiply_bitcast_fusion
  46.9 0.2 copy.20
  47.3 1.1 multiply_multiply_fusion
  48.4 0.0 all-reduce.4.cloned.1.call-update
  48.4 0.0 all-gather.3.cloned.1.call-start
  48.5 0.2 copy.19
  48.7 80.2 %all-reduce.4.cloned.1.call-done = f32[2,1,256,512]{2,3,1,0:T(8,128)} async-done(((f32[2,1,256,512]{2,3,1,0:T(8,128)}), f32[2,1,256,512]{2,3,1,0:T(8,128)}) %all-reduce.4.cloned.1.call-update) | async-done | bytes 1048592 | tf_op jit(solution)/shard_map/psum | solution.py:95
  129.0 1.9 fusion.42
  130.9 0.0 all-reduce.6.cloned.1.call-start
  131.0 0.6 dynamic_slice.19
  132.2 19.8 %all-gather.3.cloned.1.call-done = f32[1,1,512,512]{2,3,1,0:T(8,128)} async-done(((f32[1,1,256,512]{2,3,1,0:T(8,128)}), f32[1,1,512,512]{2,3,1,0:T(8,128)}) %all-gather.3.cloned.1.call-update) | async-done | bytes 1048592 | tf_op jit(solution)/shard_map/all_gather | solution.py:58
  152.0 2.1 fusion.36
  154.1 0.6 fusion.5
  154.7 0.4 collective-permute-start.4
  155.7 1.1 fusion.34
  156.8 11.4 %collective-permute-done.4 = f32[1,1,256,512]{3,2,1,0:T(8,128)S(1)} collective-permute-done((f32[1,1,256,512]{3,2,1,0:T(8,128)S(1)}, f32[1,1,256,512]{3,2,1,0:T(8,128)S(1)}, u32[]{:S(2)}, u32[]{:S(2)}) %collective-permute-start.4) | collective-permute-done | bytes 524320 | tf_op jit(solution)/shard_map/ppermute | solution.py:18
  168.2 1.3 fusion.1
  169.5 0.6 collective-permute-start.5
  170.1 12.1 %collective-permute-done.5 = f32[1,1,256,512]{3,2,1,0:T(8,128)S(1)} collective-permute-done((f32[1,1,256,512]{3,2,1,0:T(8,128)S(1)}, f32[1,1,256,512]{3,2,1,0:T(8,128)S(1)}, u32[]{:S(2)}, u32[]{:S(2)}) %collective-permute-start.5) | collective-permute-done | bytes 524320 | tf_op jit(solution)/shard_map/ppermute | solution.py:18
  182.2 2.8 select_bitcast_fusion.1
  185.1 0.0 all-gather.5.cloned.1.call-start
  185.2 1.3 collective-permute-start.6
  186.5 1.5 collective-permute-start.7
  188.0 0.2 copy.16
  188.8 69.3 %all-reduce.6.cloned.1.call-done = (bf16[1,1,256,512]{2,3,1,0:T(8,128)(2,1)}, bf16[1,1,256,512]{2,3,1,0:T(8,128)(2,1)}) async-done(((bf16[1,1,256,512]{2,3,1,0:T(8,128)(2,1)}, bf16[1,1,256,512]{2,3,1,0:T(8,128)(2,1)}), (bf16[1,1,256,512]{2,3,1,0:T(8,128)(2,1)}, bf16[1,1,256,512]{2,3,1,0:T(8,128)(2,1)})) %all-reduce.6.cloned.1.call-update) | async-done | bytes 524304 | tf_op jit(solution)/shard_map/psum | solution.py:33
  258.1 1.2 multiply_reduce_fusion
  259.3 1.0 select_reduce_fusion
  260.4 1.5 collective-permute-start.8
  262.6 1.1 compare_select_fusion
  263.7 20.2 %all-gather.5.cloned.1.call-done = f32[1,1,512,512]{2,3,1,0:T(8,128)} async-done(((f32[1,1,256,512]{2,3,1,0:T(8,128)}), f32[1,1,512,512]{2,3,1,0:T(8,128)}) %all-gather.5.cloned.1.call-update) | async-done | bytes 1048592 | tf_op jit(solution)/shard_map/all_gather | solution.py:58
  283.9 2.3 fusion.32
  286.3 1.3 fusion.2
  287.6 1.5 collective-permute-start.9
  289.1 0.1 pad_maximum_fusion
  289.2 1.0 copy.23
  290.2 1.0 fusion.30
  291.2 10.1 %collective-permute-done.9 = f32[1,1,256,512]{3,2,1,0:T(8,128)S(1)} collective-permute-done((f32[1,1,256,512]{3,2,1,0:T(8,128)S(1)}, f32[1,1,256,512]{3,2,1,0:T(8,128)S(1)}, u32[]{:S(2)}, u32[]{:S(2)}) %collective-permute-start.9) | collective-permute-done | bytes 524320 | tf_op jit(solution)/shard_map/ppermute | solution.py:18
  301.4 2.1 fusion.4
  (30 shorter events, 0.3 us)
Async XLA Ops:
  7.2 121.8 %all-reduce.4.cloned.1.call-start = ((), (), s32[]{:S(2)}) async-start(), calls=%async_computation | async-start | bytes 2097152 | tf_op jit(solution)/shard_map/psum | solution.py:95
  8.3 10.4 %collective-permute-start = (bf16[1,1,256,512]{2,3,1,0:T(8,128)(2,1)S(1)}, bf16[1,1,256,512]{2,3,1,0:T(8,128)(2,1)S(1)}, u32[]{:S(2)}, u32[]{:S(2)}) collective-permute-start(bf16[1,1,256,512]{2,3,1,0:T(8,128)(2,1)S(1)} %copy.17), channel_id=1, source_target_pairs={{0,4},{4,8},{8,12},{12,16},{16,20},{20,24},{24,28},{1,5},{5,9},{9,... | collective-permute-start | bytes 786440 | tf_op jit(solution)/shard_map/ppermute | solution.py:28
  18.7 9.1 %collective-permute-start.1 = (bf16[1,1,256,512]{2,3,1,0:T(8,128)(2,1)S(1)}, bf16[1,1,256,512]{2,3,1,0:T(8,128)(2,1)S(1)}, u32[]{:S(2)}, u32[]{:S(2)}) collective-permute-start(bf16[1,1,256,512]{2,3,1,0:T(8,128)(2,1)S(1)} %collective-permute-done), channel_id=1, source_target_pairs={{0,4},{4,8},{8,12},{12,16},{16,20},{20,24},{24,28},{1,5},{5,9},{9,... | collective-permute-start | bytes 786440 | tf_op jit(solution)/shard_map/ppermute | solution.py:28
  27.8 8.3 %collective-permute-start.2 = (bf16[1,1,256,512]{2,3,1,0:T(8,128)(2,1)S(1)}, bf16[1,1,256,512]{2,3,1,0:T(8,128)(2,1)S(1)}, u32[]{:S(2)}, u32[]{:S(2)}) collective-permute-start(bf16[1,1,256,512]{2,3,1,0:T(8,128)(2,1)S(1)} %collective-permute-done.1), channel_id=1, source_target_pairs={{0,4},{4,8},{8,12},{12,16},{16,20},{20,24},{24,28},{1,5},{5,9},{9,... | collective-permute-start | bytes 786440 | tf_op jit(solution)/shard_map/ppermute | solution.py:28
  36.1 11.1 %collective-permute-start.3 = (bf16[1,1,256,512]{2,3,1,0:T(8,128)(2,1)S(1)}, bf16[1,1,256,512]{2,3,1,0:T(8,128)(2,1)S(1)}, u32[]{:S(2)}, u32[]{:S(2)}) collective-permute-start(bf16[1,1,256,512]{2,3,1,0:T(8,128)(2,1)S(1)} %collective-permute-done.2), channel_id=1, source_target_pairs={{0,4},{4,8},{8,12},{12,16},{16,20},{20,24},{24,28},{1,5},{5,9},{9,... | collective-permute-start | bytes 786440 | tf_op jit(solution)/shard_map/ppermute | solution.py:28
  47.3 1.2 copy-start.4
  48.4 103.6 %all-gather.3.cloned.1.call-start = ((), (), s32[]{:S(2)}) async-start(), calls=%async_computation.1 | async-start | bytes 1572864 | tf_op jit(solution)/shard_map/all_gather | solution.py:58
  48.7 82.3 %copy-start.6 = (s32[2]{0:T(128)S(1)}, s32[2]{0:T(128)}, u32[]{:S(2)}) copy-start(s32[2]{0:T(128)} %param.17) | copy-start | bytes 28
  130.9 127.2 %all-reduce.6.cloned.1.call-start = ((), (), s32[]{:S(2)}) async-start(), calls=%async_computation.3 | async-start | bytes 1048576 | tf_op jit(solution)/shard_map/psum | solution.py:33
  152.0 3.7 %copy-start = (f32[1,1,512,512]{2,3,1,0:T(8,128)S(1)}, f32[1,1,512,512]{2,3,1,0:T(8,128)}, u32[]{:S(2)}) copy-start(f32[1,1,512,512]{2,3,1,0:T(8,128)} %all-gather.3.cloned.1.call-done) | copy-start | bytes 3145732
  154.7 13.6 %collective-permute-start.4 = (f32[1,1,256,512]{3,2,1,0:T(8,128)S(1)}, f32[1,1,256,512]{3,2,1,0:T(8,128)S(1)}, u32[]{:S(2)}, u32[]{:S(2)}) collective-permute-start(f32[1,1,256,512]{3,2,1,0:T(8,128)S(1)} %bitcast.91), channel_id=1, source_target_pairs={{0,1},{1,0},{2,3},{3,2},{4,5},{5,4},{6,7},{7,6},{8,9},{9,8},{10,11... | collective-permute-start | bytes 1572872 | tf_op jit(solution)/shard_map/ppermute | solution.py:18
  169.5 12.7 %collective-permute-start.5 = (f32[1,1,256,512]{3,2,1,0:T(8,128)S(1)}, f32[1,1,256,512]{3,2,1,0:T(8,128)S(1)}, u32[]{:S(2)}, u32[]{:S(2)}) collective-permute-start(f32[1,1,256,512]{3,2,1,0:T(8,128)S(1)} %fusion.1), channel_id=1, source_target_pairs={{0,1},{1,0},{2,3},{3,2},{4,5},{5,4},{6,7},{7,6},{8,9},{9,8},{10,11... | collective-permute-start | bytes 1572872 | tf_op jit(solution)/shard_map/ppermute | solution.py:18
  170.1 17.8 %copy-start.5 = (f32[1,256,512]{2,1,0:T(8,128)S(1)}, f32[1,256,512]{2,1,0:T(8,128)}, u32[]{:S(2)}) copy-start(f32[1,256,512]{2,1,0:T(8,128)} %param.14) | copy-start | bytes 1572868
  185.1 98.8 %all-gather.5.cloned.1.call-start = ((), (), s32[]{:S(2)}) async-start(), calls=%async_computation.2 | async-start | bytes 1572864 | tf_op jit(solution)/shard_map/all_gather | solution.py:58
  185.2 74.2 %collective-permute-start.6 = (bf16[1,1,256,512]{2,3,1,0:T(8,128)(2,1)S(1)}, bf16[1,1,256,512]{2,3,1,0:T(8,128)(2,1)S(1)}, u32[]{:S(2)}, u32[]{:S(2)}) collective-permute-start(bf16[1,1,256,512]{2,3,1,0:T(8,128)(2,1)S(1)} %copy.17), channel_id=1, source_target_pairs={{0,2},{1,3},{4,6},{5,7},{8,10},{9,11},{12,14},{13,15},{16,18},{17,... | collective-permute-start | bytes 786440 | tf_op jit(solution)/shard_map/ppermute | solution.py:43
  186.5 72.9 %collective-permute-start.7 = (bf16[1,1,256,512]{2,3,1,0:T(8,128)(2,1)S(1)}, bf16[1,1,256,512]{2,3,1,0:T(8,128)(2,1)S(1)}, u32[]{:S(2)}, u32[]{:S(2)}) collective-permute-start(bf16[1,1,256,512]{2,3,1,0:T(8,128)(2,1)S(1)} %copy.17), channel_id=1, source_target_pairs={{2,0},{3,1},{6,4},{7,5},{10,8},{11,9},{14,12},{15,13},{18,16},{19,... | collective-permute-start | bytes 786440 | tf_op jit(solution)/shard_map/ppermute | solution.py:44
  260.4 25.8 %collective-permute-start.8 = (f32[1,1,256,512]{2,3,1,0:T(8,128)S(1)}, f32[1,1,256,512]{2,3,1,0:T(8,128)S(1)}, u32[]{:S(2)}, u32[]{:S(2)}) collective-permute-start(f32[1,1,256,512]{2,3,1,0:T(8,128)S(1)} %fusion.43), channel_id=1, source_target_pairs={{0,1},{1,0},{2,3},{3,2},{4,5},{5,4},{6,7},{7,6},{8,9},{9,8},{10,11... | collective-permute-start | bytes 1572872 | tf_op jit(solution)/shard_map/ppermute | solution.py:18
  286.2 2.9 copy-start.2
  286.3 2.9 copy-start.3
  287.6 2.6 copy-start.1
  287.6 13.8 %collective-permute-start.9 = (f32[1,1,256,512]{3,2,1,0:T(8,128)S(1)}, f32[1,1,256,512]{3,2,1,0:T(8,128)S(1)}, u32[]{:S(2)}, u32[]{:S(2)}) collective-permute-start(f32[1,1,256,512]{3,2,1,0:T(8,128)S(1)} %bitcast.93), channel_id=1, source_target_pairs={{0,1},{1,0},{2,3},{3,2},{4,5},{5,4},{6,7},{7,6},{8,9},{9,8},{10,11... | collective-permute-start | bytes 1572872 | tf_op jit(solution)/shard_map/ppermute | solution.py:18
Sparse Core Ops, SparseCore 0:
  48.5 80.3 all-reduce.3
  131.1 20.8 all-gather.2
  185.2 72.8 all-reduce.5
  260.5 23.3 all-gather.4
